TPU v7x, 512 devices: a whole 4x4x16 slice. The times are simulated.
512 devices in a mesh: dp: 4 (over x), cand: 32 (over z, core), tensor: 4 (over y).
Axes of the slice: x: 4, y: 4, z: 16, core: 2. Of those that a mesh axis runs over, the one named last changes fastest.
Arguments:
- context: bfloat16 [8, 4096, 3584], P('dp', 'cand', 'tensor'), may hold values from -12 to 12
- residual: bfloat16 [8, 4096, 3584], P('dp', ('cand', 'tensor')), may hold values from -36 to 36
- out_weight: bfloat16 [3584, 3584], P('cand', 'tensor'), may hold values from -0.09375 to 0.09375
- adapter_down: bfloat16 [3584, 16], P('tensor'), may hold values from -0.09375 to 0.09375
- adapter_up_weight: bfloat16 [16, 3584], replicated, may hold values from -1.5 to 1.5
- norm_gain: float32 [3584], replicated, may hold values from 0.5 to 1.5
- score_weight: float32 [3584], replicated, may hold values from -0.09375 to 0.09375
- teacher: bfloat16 [8, 4096, 4096], P('dp', 'cand', 'tensor'), may hold values from 0.019897461 to 0.9765625
- pair_mask: int32 [8, 4096, 4096], P('dp', 'cand', 'tensor'), may hold values from 0 to 1, as said below
- loss_scale: float32 [8], P('dp'), may hold values from 65536 to 262144
Outputs:
- context_grad: bfloat16 [8, 4096, 3584], P('dp', 'cand', 'tensor')
- residual_gradient: bfloat16 [8, 4096, 3584], P('dp', ('cand', 'tensor'))
- down_grad: float32 [3584, 16], P('tensor')
- up_weight_gradient: float32 [16, 3584], P(None, 'tensor')
- pair_loss: float32 [8], P('dp')
Inputs may be any that keep to these rules, and one draw needn't show every extreme that they name: pair_mask holds 0 or 1; with P = 32, every pair (i, j) whose group j // P lies 4096 / (2P) groups after i // P, counted round over the 4096 / P groups, is valid.
All inputs are finite; a program needn't handle non-finite values.
Results may differ from a plain program's by a relative error of at most 0.02.
Values may be sent and summed in bfloat16 or wider, within the bound.
No kernel may reach another device: no remote copies, remote signals or barrier semaphores. Data moves between devices by JAX's collectives and lax.ppermute only.
A program may use at most 64 MiB of HBM per device.

v0:
```python
import jax
import jax.numpy as jnp
from jax import lax
from jax.sharding import PartitionSpec as P

ADAPTER_SCALE = 0.5
epsilon = 1e-06
F32 = jnp.float32
BF16 = jnp.bfloat16


def on_device(
    context,
    residual,
    out_weight,
    adapter_down,
    adapter_up_weight,
    norm_gain,
    score_weight,
    teacher,
    pair_mask,
    loss_scale,
):
    queries, cand_rows, _ = context.shape
    width = residual.shape[2]
    cols = teacher.shape[2]
    tensor_count = lax.axis_size("tensor")
    cand_count = lax.axis_size("cand")
    share = cand_rows // tensor_count
    near = cols // cand_rows
    tensor_index = lax.axis_index("tensor")
    dp_index = lax.axis_index("dp")
    full_weight = lax.all_gather(out_weight, "cand", axis=0, tiled=True)
    low_terms = jnp.einsum("qch,hr->qcr", context, adapter_down, preferred_element_type=F32).astype(
        BF16
    )
    low_all = lax.all_gather(low_terms, "tensor", axis=0)
    adapter_in = jnp.sum(low_all.astype(F32), axis=0).astype(BF16)
    adapter_own = lax.dynamic_slice_in_dim(adapter_in, tensor_index * share, share, 1)
    lifted = jnp.einsum("qcr,rd->qcd", adapter_own, adapter_up_weight, preferred_element_type=F32)
    base = residual.astype(F32) + ADAPTER_SCALE * lifted
    valid = pair_mask.astype(F32)
    target = teacher.astype(F32)
    mask_count = jnp.sum(valid, axis=(1, 2))
    row_known = jnp.sum(valid * target, axis=2)
    col_known = jnp.sum(valid * (1.0 - target), axis=1)
    groups = [[a * near + b for b in range(near)] for a in range(cand_count // near)]
    swap = [
        ((a * near + b) * tensor_count + t, (t * near + b) * tensor_count + a)
        for a in range(cand_count // near)
        for b in range(near)
        for t in range(tensor_count)
    ]
    blocks = jnp.swapaxes(pair_mask.astype(BF16).reshape(queries, cand_rows, near, cand_rows), 1, 2)
    blocks = jnp.swapaxes(blocks, 2, 3)
    blocks = jnp.swapaxes(blocks, 0, 1)
    blocks = lax.all_to_all(blocks, "cand", 0, 0, axis_index_groups=groups, tiled=True)
    blocks = lax.ppermute(blocks, ("cand", "tensor"), swap)
    other_valid = jnp.moveaxis(blocks, 0, 2).reshape(queries, cand_rows, cols)
    col_known = jnp.swapaxes(col_known.reshape(queries, near, cand_rows), 0, 1)
    col_known = lax.all_to_all(col_known, "cand", 0, 0, axis_index_groups=groups, tiled=True)
    col_known = lax.ppermute(jnp.sum(col_known, axis=0), ("cand", "tensor"), swap)
    both = valid + other_valid.astype(F32)
    known = row_known + col_known
    full_weight, adapter_in, base, both, known, mask_count = lax.optimization_barrier(
        (full_weight, adapter_in, base, both, known, mask_count)
    )
    by_owner = jnp.swapaxes(context.reshape(queries, tensor_count, share, context.shape[2]), 0, 1)
    head_terms = jnp.einsum(
        "tqch,dh->tqcd", by_owner, full_weight, preferred_element_type=F32
    ).astype(BF16)
    head_terms = lax.all_to_all(head_terms, "tensor", 0, 0, tiled=True)
    hidden = (base + jnp.sum(head_terms.astype(F32), axis=0)).astype(BF16).astype(F32)
    inv_rms = lax.rsqrt(jnp.mean(hidden * hidden, axis=2) + epsilon)
    gain = norm_gain * score_weight
    dot = jnp.sum(hidden * gain, axis=2)
    scores = dot * inv_rms
    slant = inv_rms * inv_rms * dot / width
    unit = inv_rms[:, :, None] * (gain - hidden * slant[:, :, None])
    unit_sent, unit, scores = lax.optimization_barrier((unit.astype(BF16), unit, scores))
    unit_all = lax.all_gather(unit_sent, "tensor", axis=1, tiled=True)
    message = jnp.concatenate([scores, mask_count[:, None]], axis=1)
    message = lax.all_gather(message, "tensor", axis=0)
    own_scores = jnp.swapaxes(message[:, :, :share], 0, 1).reshape(queries, cand_rows)
    message = jnp.concatenate([own_scores, jnp.sum(message[:, :, share], axis=0)[:, None]], axis=1)
    message = lax.all_gather(message, "cand", axis=0)
    count = jnp.sum(message[:, :, cand_rows], axis=0)
    col_scores = lax.dynamic_slice_in_dim(message, tensor_index * near, near, 0)
    col_scores = jnp.swapaxes(col_scores[:, :, :cand_rows], 0, 1).reshape(queries, cols)
    margin = own_scores[:, :, None] - col_scores[:, None, :]
    raw = jnp.sum(both * jax.nn.sigmoid(margin), axis=2) - known
    total = jnp.sum(valid * (jax.nn.softplus(margin) - target * margin), axis=(1, 2))
    sums = lax.psum(jnp.concatenate([raw, total[:, None]], axis=1), "tensor")
    score_grad = sums[:, :cand_rows] * (loss_scale / count)[:, None]
    own_grad = lax.dynamic_slice_in_dim(score_grad, tensor_index * share, share, 1)
    grad_rows = (own_grad[:, :, None] * unit).astype(BF16)
    adapter_unit = ADAPTER_SCALE * jnp.einsum(
        "qcd,rd->qcr", unit_all, adapter_up_weight, preferred_element_type=F32
    )
    context_unit = jnp.einsum(
        "qcd,dh->qch", unit_all, full_weight, preferred_element_type=F32
    ) + jnp.einsum(
        "qcr,hr->qch", adapter_unit.astype(BF16), adapter_down, preferred_element_type=F32
    )
    context_grad = (score_grad[:, :, None] * context_unit).astype(BF16)
    adapter_back = (score_grad[:, :, None] * adapter_unit).astype(BF16)
    down_local = jnp.einsum("qcr,qch->rh", adapter_back, context, preferred_element_type=F32)
    block = lax.dynamic_slice_in_dim(unit_all, tensor_index * context.shape[2], context.shape[2], 2)
    block = (score_grad[:, :, None] * block.astype(F32)).astype(BF16)
    up_local = ADAPTER_SCALE * jnp.einsum(
        "qcr,qcd->rd", adapter_in, block, preferred_element_type=F32
    )
    slots = jnp.zeros((128,), F32)
    slots = lax.dynamic_update_slice_in_dim(slots, sums[:, cand_rows], dp_index * queries, 0)
    flat = jnp.concatenate([down_local, up_local], axis=0)
    columns = flat.shape[1]
    flat = jnp.concatenate([flat, jnp.broadcast_to(slots, (flat.shape[0], 128))], axis=1)
    pieces = lax.all_to_all(flat, "cand", 0, 0, tiled=True)
    piece = jnp.sum(pieces.reshape(cand_count, -1, flat.shape[1]), axis=0)
    piece = lax.psum(piece, "dp")
    flat = lax.all_gather(piece[:, :columns], "cand", axis=0, tiled=True)
    rank = adapter_down.shape[1]
    down_grad = flat[:rank].T
    up_weight_gradient = flat[rank:]
    loss_sum = lax.dynamic_slice_in_dim(piece[0, columns:], dp_index * queries, queries, 0)
    pair_loss = loss_sum / count
    return (context_grad, grad_rows, down_grad, up_weight_gradient, pair_loss)


def solution(mesh):
    in_specs = (
        P("dp", "cand", "tensor"),
        P("dp", ("cand", "tensor"), None),
        P("cand", "tensor"),
        P("tensor", None),
        P(),
        P(),
        P(),
        P("dp", "cand", "tensor"),
        P("dp", "cand", "tensor"),
        P("dp"),
    )
    out_specs = (
        P("dp", "cand", "tensor"),
        P("dp", ("cand", "tensor"), None),
        P("tensor", None),
        P(None, "tensor"),
        P("dp"),
    )
    return jax.shard_map(
        on_device, mesh=mesh, in_specs=in_specs, out_specs=out_specs, check_vma=False
    )
```

profile of v0, /device:TPU:1, one launch (start us, length us, event | category | flops | bytes accessed | tf_op | source)
XLA Modules:
  0.0 317.1 jit_solution(14492580790109656171)
XLA Ops:
  7.2 0.7 all-gather.9.cloned.1.call-update
  7.9 1.5 copy.36
  9.6 0.3 copy.38
  9.8 23.6 %all_to_all.24 = bf16[8,2,128,128]{2,3,1,0:T(8,128)(2,1)S(1)} all-to-all(bf16[8,2,128,128]{2,3,1,0:T(8,128)(2,1)S(1)} %copy.38), channel_id=1, replica_groups={{0,4,8,12,16,20,24,28},{32,36,40,44,48,52,56,60},{64,68,72,76,80,84,88,..., dimensions={0} | all-to-all | bytes 1048576 | tf_op jit(solution)/shard_map/all_to_all | solution.py:57
  33.5 0.9 copy.39
  34.3 1.7 collective-permute-start
  36.0 0.3 copy.40
  36.3 2.0 fusion.23
  38.3 4.3 %all-to-all-start.1 = ((f32[8,2,128]{2,1,0:T(2,128)}), f32[8,2,128]{2,1,0:T(2,128)S(1)}, u32[]{:S(2)}, u32[]{:S(2)}) async-start(f32[8,2,128]{2,1,0:T(2,128)} %bitcast.8), calls=%async_computation.1 | async-start | bytes 16384 | tf_op jit(solution)/shard_map/all_to_all | solution.py:61
  42.6 0.2 convolution_convert_fusion
  42.8 94.4 %all-gather = bf16[8,128,16]{1,2,0:T(8,128)(2,1)S(1)} all-gather(bf16[2,128,16]{1,2,0:T(8,128)(2,1)S(1)} %convolution_convert_fusion), channel_id=2, replica_groups=mesh['dp'=4,'cand'=32,'tensor'=4] {'tensor'}, dimensions={0}, use_global_device_ids=true | all-gather | bytes 40960 | tf_op jit(solution)/shard_map/all_gather | solution.py:37
  137.3 0.7 collective-permute-start.1
  137.9 1.3 fusion.10
  139.2 11.5 %all-gather.9.cloned.1.call-done = bf16[3584,896]{1,0:T(8,128)(2,1)} async-done(((bf16[112,896]{1,0:T(8,128)(2,1)}), bf16[3584,896]{1,0:T(8,128)(2,1)}) %all-gather.9.cloned.1.call-update) | async-done | bytes 6422544 | tf_op jit(solution)/shard_map/all_gather | solution.py:33
  150.8 6.2 %fusion.7 = bf16[4,2,32,3584]{3,2,1,0:T(8,128)(2,1)} fusion(bf16[3584,896]{1,0:T(8,128)(2,1)} %all-gather.9.cloned.1.call-done, bf16[2,4,32,896]{3,2,1,0:T(8,128)(2,1)S(1)} %bitcast.85), kind=kOutput, calls=%fused_computation.5 | convolution fusion | flops 1645084672 | bytes 8716288 | tf_op jit(solution)/shard_map/tqch,dh->tqcd/dot_general | solution.py:69
  156.9 6.8 %all-to-all-start.2 = ((bf16[4,2,32,3584]{3,2,1,0:T(8,128)(2,1)}), bf16[4,2,32,3584]{3,2,1,0:T(8,128)(2,1)S(1)}, u32[]{:S(2)}, u32[]{:S(2)}) async-start(bf16[4,2,32,3584]{3,2,1,0:T(8,128)(2,1)} %fusion.7), calls=%async_computation.2 | async-start | bytes 3670016 | tf_op jit(solution)/shard_map/all_to_all | solution.py:72
  163.7 0.7 mul.141
  164.4 22.3 %all-to-all-done.2 = bf16[4,2,32,3584]{3,2,1,0:T(8,128)(2,1)S(1)} async-done(((bf16[4,2,32,3584]{3,2,1,0:T(8,128)(2,1)}), bf16[4,2,32,3584]{3,2,1,0:T(8,128)(2,1)S(1)}, u32[]{:S(2)}, u32[]{:S(2)}) %all-to-all-start.2) | async-done | bytes 1835040 | tf_op jit(solution)/shard_map/all_to_all | solution.py:72
  186.7 0.3 convert_reduce_fusion
  187.0 0.9 copy-done.2
  187.9 0.3 fusion.36
  188.2 1.3 fusion.39
  189.5 0.1 copy.43
  189.7 6.1 %all-gather.3 = f32[4,2,33]{2,1,0:T(2,128)S(1)} all-gather(f32[1,2,33]{2,1,0:T(2,128)S(1)} %maximum_bitcast_fusion.2), channel_id=3, replica_groups=mesh['dp'=4,'cand'=32,'tensor'=4] {'tensor'}, dimensions={0}, use_global_device_ids=true | all-gather | bytes 1320 | tf_op jit(solution)/shard_map/all_gather | solution.py:83
  195.8 0.1 sub.37
  195.9 0.2 slice_reduce_fusion.1
  196.0 0.1 copy.45
  196.2 34.2 %all-gather.4 = f32[32,2,129]{2,1,0:T(2,128)S(1)} all-gather(f32[1,2,129]{2,1,0:T(2,128)S(1)} %maximum_bitcast_fusion.1), channel_id=4, replica_groups=mesh['dp'=4,'cand'=32,'tensor'=4] {'cand'}, dimensions={0}, use_global_device_ids=true | all-gather | bytes 34056 | tf_op jit(solution)/shard_map/all_gather | solution.py:86
  230.4 1.1 fusion.35
  231.5 0.1 copy.47
  231.6 0.1 slice_reduce_fusion
  231.8 6.6 %psum.14 = f32[2,129]{1,0:T(2,128)S(1)} all-reduce(f32[2,129]{1,0:T(2,128)S(1)} %pad_maximum_fusion), channel_id=1, replica_groups=mesh['dp'=4,'cand'=32,'tensor'=4] {'tensor'}, use_global_device_ids=true, to_apply=%region_11.12 | all-reduce | flops 258 | bytes 2064 | tf_op jit(solution)/shard_map/psum | solution.py:93
  238.4 0.1 slice_reduce_fusion.2
  238.5 0.2 dynamic_update_slice.3
  238.9 2.1 multiply_convert_fusion.1
  241.0 2.2 fusion.44
  243.2 0.4 fusion.48
  243.6 0.2 convolution_bitcast_fusion.1
  243.7 0.3 fusion.20
  244.1 0.8 copy.48
  244.8 9.0 %all-to-all-start.3 = ((f32[32,1,1024]{2,1,0:T(1,128)}), f32[32,1,1024]{2,1,0:T(1,128)S(1)}, u32[]{:S(2)}, u32[]{:S(2)}) async-start(f32[32,1,1024]{2,1,0:T(1,128)} %copy.48), calls=%async_computation.3 | async-start | bytes 262144 | tf_op jit(solution)/shard_map/all_to_all | solution.py:118
  253.8 5.7 %fusion.17 = bf16[2,128,896]{2,1,0:T(8,128)(2,1)} fusion(f32[2,128,896]{2,1,0:T(8,128)S(1)} %fusion.48, bf16[2,128,3584]{2,1,0:T(8,128)(2,1)S(1)} %copy-done.3, bf16[3584,896]{1,0:T(8,128)(2,1)} %all-gather.9.cloned.1.call-done, f32[2,128]{1,0:T(2,128)S(1)} %get-tuple-element.31), kind=kOutput, calls=%fused_computation.22 | convolution fusion | flops 1644855296 | bytes 9634816 | tf_op jit(solution)/shard_map/qcd,dh->qch/dot_general | solution.py:100
  259.5 10.2 %all-to-all-done.3 = f32[32,1,1024]{2,1,0:T(1,128)S(1)} async-done(((f32[32,1,1024]{2,1,0:T(1,128)}), f32[32,1,1024]{2,1,0:T(1,128)S(1)}, u32[]{:S(2)}, u32[]{:S(2)}) %all-to-all-start.3) | async-done | bytes 131104 | tf_op jit(solution)/shard_map/all_to_all | solution.py:118
  269.7 0.1 reduce_sum.134
  269.8 8.4 %psum.15 = f32[1,1024]{1,0:T(1,128)S(1)} all-reduce(f32[1,1024]{1,0:T(1,128)S(1)} %bitcast.87), channel_id=1, replica_groups=mesh['dp'=4,'cand'=32,'tensor'=4] {'dp'}, use_global_device_ids=true, to_apply=%region_14.15 | all-reduce | flops 1024 | bytes 8192 | tf_op jit(solution)/shard_map/psum | solution.py:120
  278.2 0.6 fusion.57
  278.8 30.8 %all-gather.5 = f32[32,1,896]{2,1,0:T(1,128)S(1)} all-gather(f32[1,1,896]{2,1,0:T(1,128)S(1)} %slice_bitcast_fusion.1), channel_id=1, replica_groups=mesh['dp'=4,'cand'=32,'tensor'=4] {'cand'}, dimensions={0}, use_global_device_ids=true | all-gather | bytes 118272 | tf_op jit(solution)/shard_map/all_gather | solution.py:121
  309.6 0.6 copy_bitcast_fusion
  (49 shorter events, 0.6 us)
Async XLA Ops:
  7.2 130.8 %copy-start = (bf16[16,3584]{1,0:T(8,128)(2,1)S(1)}, bf16[16,3584]{1,0:T(8,128)(2,1)}, u32[]{:S(2)}) copy-start(bf16[16,3584]{1,0:T(8,128)(2,1)} %param.14) | copy-start | bytes 344068
  7.2 143.6 %all-gather.9.cloned.1.call-start = ((), (), s32[]{:S(2)}) async-start(), calls=%async_computation.4 | async-start | bytes 6623232 | tf_op jit(solution)/shard_map/all_gather | solution.py:33
  9.6 26.5 %copy-start.6 = (bf16[2,128,1024]{2,1,0:T(8,128)(2,1)S(1)}, bf16[2,128,1024]{2,1,0:T(8,128)(2,1)}, u32[]{:S(2)}) copy-start(bf16[2,128,1024]{2,1,0:T(8,128)(2,1)} %param.17) | copy-start | bytes 1572868
  34.3 2.0 collective-permute-start
  36.3 6.3 %copy-start.4 = (bf16[2,128,896]{2,1,0:T(8,128)(2,1)S(1)}, bf16[2,128,896]{2,1,0:T(8,128)(2,1)}, u32[]{:S(2)}) copy-start(bf16[2,128,896]{2,1,0:T(8,128)(2,1)} %param.10) | copy-start | bytes 1376260
  36.3 6.3 %copy-start.8 = (bf16[896,16]{0,1:T(8,128)(2,1)S(1)}, bf16[896,16]{0,1:T(8,128)(2,1)}, u32[]{:S(2)}) copy-start(bf16[896,16]{0,1:T(8,128)(2,1)} %param.13) | copy-start | bytes 86020
  36.3 101.6 %copy-start.7 = (bf16[2,32,3584]{2,1,0:T(8,128)(2,1)S(1)}, bf16[2,32,3584]{2,1,0:T(8,128)(2,1)}, u32[]{:S(2)}) copy-start(bf16[2,32,3584]{2,1,0:T(8,128)(2,1)} %param.11) | copy-start | bytes 1376260
  38.3 98.9 %all-to-all-start.1 = ((f32[8,2,128]{2,1,0:T(2,128)}), f32[8,2,128]{2,1,0:T(2,128)S(1)}, u32[]{:S(2)}, u32[]{:S(2)}) async-start(f32[8,2,128]{2,1,0:T(2,128)} %bitcast.8), calls=%async_computation.1 | async-start | bytes 16384 | tf_op jit(solution)/shard_map/all_to_all | solution.py:61
  137.3 2.0 collective-permute-start.1
  156.9 29.8 %all-to-all-start.2 = ((bf16[4,2,32,3584]{3,2,1,0:T(8,128)(2,1)}), bf16[4,2,32,3584]{3,2,1,0:T(8,128)(2,1)S(1)}, u32[]{:S(2)}, u32[]{:S(2)}) async-start(bf16[4,2,32,3584]{3,2,1,0:T(8,128)(2,1)} %fusion.7), calls=%async_computation.2 | async-start | bytes 3670016 | tf_op jit(solution)/shard_map/all_to_all | solution.py:72
  163.7 77.3 %all-gather.11.cloned.1.call-start = ((), (), s32[]{:S(2)}) async-start(), calls=%async_computation.5 | async-start | bytes 2293760 | tf_op jit(solution)/shard_map/all_gather | solution.py:81
  186.7 1.2 copy-start.2
  187.9 42.5 %copy-start.1 = (f32[2,128,1024]{1,2,0:T(8,128)S(1)}, f32[2,128,1024]{1,2,0:T(8,128)}, u32[]{:S(2)}) copy-start(f32[2,128,1024]{1,2,0:T(8,128)} %get-tuple-element.14) | copy-start | bytes 3145732
  189.5 42.3 %copy-start.10 = (f32[2]{0:T(128)S(1)}, f32[2]{0:T(128)}, u32[]{:S(2)}) copy-start(f32[2]{0:T(128)} %param.19) | copy-start | bytes 28
  231.5 11.7 %copy-start.9 = (bf16[896,16]{0,1:T(8,128)(2,1)S(1)}, bf16[896,16]{0,1:T(8,128)(2,1)}, u32[]{:S(2)}) copy-start(bf16[896,16]{0,1:T(8,128)(2,1)} %param.13) | copy-start | bytes 86020
  238.9 4.7 %copy-start.5 = (bf16[2,128,896]{2,1,0:T(8,128)(2,1)S(1)}, bf16[2,128,896]{2,1,0:T(8,128)(2,1)}, u32[]{:S(2)}) copy-start(bf16[2,128,896]{2,1,0:T(8,128)(2,1)} %param.10) | copy-start | bytes 1376260
  241.0 2.7 copy-start.3
  244.8 24.9 %all-to-all-start.3 = ((f32[32,1,1024]{2,1,0:T(1,128)}), f32[32,1,1024]{2,1,0:T(1,128)S(1)}, u32[]{:S(2)}, u32[]{:S(2)}) async-start(f32[32,1,1024]{2,1,0:T(1,128)} %copy.48), calls=%async_computation.3 | async-start | bytes 262144 | tf_op jit(solution)/shard_map/all_to_all | solution.py:118
Sparse Core Ops, SparseCore 0:
  10.1 140.5 all-gather.8
  189.6 34.0 all-gather.10
where the time goes:
time: 318 us; the launch traced here: 317 us
  blocking collectives  204 us (64%)
  waiting for transfers between devices  44.7 us (14%)
  starting transfers between devices  22.4 us (7%)
  matrix products  16.3 us (5%)
  between operations  14.2 us (4%)
  other arithmetic  9.15 us (3%)
  local copies, waits for them, and re-layouts  6.21 us (2%)
    all_gather x1, blocking collectives, on_device(): low_all = lax.all_gather(low_terms, 'tensor', axis=0)  94.4 us
    all_gather x1, blocking collectives, on_device(): message = lax.all_gather(message, 'cand', axis=0)  34.2 us
    all_gather x1, blocking collectives, on_device(): flat = lax.all_gather(piece[:, :columns], 'cand', axis=0, tiled=True)  30.8 us
    all_to_all x1, blocking collectives, on_device(): lax.all_to_all(blocks, 'cand', 0, 0, axis_index_groups=groups, tiled=True)  23.6 us
    all_to_all x1, waiting for transfers between devices, on_device(): head_terms = lax.all_to_all(head_terms, 'tensor', 0, 0, tiled=True)  22.3 us
    all_gather x1, waiting for transfers between devices, on_device(): full_weight = lax.all_gather(out_weight, 'cand', axis=0, tiled=True)  11.5 us
    all_to_all x1, waiting for transfers between devices, on_device(): pieces = lax.all_to_all(flat, 'cand', 0, 0, tiled=True)  10.2 us
    all_to_all x1, starting transfers between devices, on_device(): pieces = lax.all_to_all(flat, 'cand', 0, 0, tiled=True)  9 us
  transfers between devices with their start and end apart: 7, of which 3 were waited for; matrix products, arithmetic and copies ran while one was open for 6% of the time, Pallas kernels for 0%

commit v1 on v0

--- a/solution.py
+++ b/solution.py
@@ -117,7 +117,7 @@
     flat = jnp.concatenate([flat, jnp.broadcast_to(slots, (flat.shape[0], 128))], axis=1)
     pieces = lax.all_to_all(flat, "cand", 0, 0, tiled=True)
     piece = jnp.sum(pieces.reshape(cand_count, -1, flat.shape[1]), axis=0)
-    piece = lax.psum(piece, "dp")
+    piece = jnp.sum(lax.all_gather(piece, "dp"), axis=0)
     flat = lax.all_gather(piece[:, :columns], "cand", axis=0, tiled=True)
     rank = adapter_down.shape[1]
     down_grad = flat[:rank].T

time: 318 us -> 320 us (level)
    all_gather x0 -> x1, blocking collectives: none -> 9.4 us  [on_device(): piece = jnp.sum(lax.all_gather(piece, 'dp'), axis=0)]
    psum x1 -> x0, blocking collectives: 8.39 us -> none  [on_device(): piece = lax.psum(piece, 'dp')]
  transfers between devices with their start and end apart: 7 -> 7, of which waited for: 3 -> 3; matrix products, arithmetic and copies ran while one was open for 6% -> 5% of each run, Pallas kernels for 0% -> 0%
where the time goes in v1:
time: 320 us; the launch traced here: 319 us
  blocking collectives  206 us (64%)
  waiting for transfers between devices  44.5 us (14%)
  starting transfers between devices  22.5 us (7%)
  matrix products  16.3 us (5%)
  between operations  14.3 us (4%)
  other arithmetic  9.17 us (3%)
  local copies, waits for them, and re-layouts  6.21 us (2%)
    all_gather x1, blocking collectives, on_device(): low_all = lax.all_gather(low_terms, 'tensor', axis=0)  94.4 us
    all_gather x1, blocking collectives, on_device(): message = lax.all_gather(message, 'cand', axis=0)  34.3 us
    all_gather x1, blocking collectives, on_device(): flat = lax.all_gather(piece[:, :columns], 'cand', axis=0, tiled=True)  31.7 us
    all_to_all x1, blocking collectives, on_device(): lax.all_to_all(blocks, 'cand', 0, 0, axis_index_groups=groups, tiled=True)  23.6 us
    all_to_all x1, waiting for transfers between devices, on_device(): head_terms = lax.all_to_all(head_terms, 'tensor', 0, 0, tiled=True)  22.2 us
    all_gather x1, waiting for transfers between devices, on_device(): full_weight = lax.all_gather(out_weight, 'cand', axis=0, tiled=True)  11.4 us
    all_to_all x1, waiting for transfers between devices, on_device(): pieces = lax.all_to_all(flat, 'cand', 0, 0, tiled=True)  10.2 us
    all_gather x1, blocking collectives, on_device(): piece = jnp.sum(lax.all_gather(piece, 'dp'), axis=0)  9.4 us
  transfers between devices with their start and end apart: 7, of which 3 were waited for; matrix products, arithmetic and copies ran while one was open for 5% of the time, Pallas kernels for 0%

profile of v1, /device:TPU:1, one launch (start us, length us, event | category | flops | bytes accessed | tf_op | source)
XLA Modules:
  0.0 319.0 jit_solution(451481984941035531)
XLA Ops:
  7.2 0.7 all-gather.10.cloned.1.call-update
  7.9 1.5 copy.49
  9.6 0.3 copy.51
  9.8 23.6 %all_to_all.24 = bf16[8,2,128,128]{2,3,1,0:T(8,128)(2,1)S(1)} all-to-all(bf16[8,2,128,128]{2,3,1,0:T(8,128)(2,1)S(1)} %copy.51), channel_id=1, replica_groups={{0,4,8,12,16,20,24,28},{32,36,40,44,48,52,56,60},{64,68,72,76,80,84,88,..., dimensions={0} | all-to-all | bytes 1048576 | tf_op jit(solution)/shard_map/all_to_all | solution.py:57
  33.5 0.8 copy.52
  34.3 1.7 collective-permute-start
  36.0 0.3 copy.53
  36.3 2.0 fusion.23
  38.3 4.3 %all-to-all-start.1 = ((f32[8,2,128]{2,1,0:T(2,128)}), f32[8,2,128]{2,1,0:T(2,128)S(1)}, u32[]{:S(2)}, u32[]{:S(2)}) async-start(f32[8,2,128]{2,1,0:T(2,128)} %bitcast.8), calls=%async_computation.1 | async-start | bytes 16384 | tf_op jit(solution)/shard_map/all_to_all | solution.py:61
  42.6 0.2 convolution_convert_fusion
  42.8 94.4 %all-gather = bf16[8,128,16]{1,2,0:T(8,128)(2,1)S(1)} all-gather(bf16[2,128,16]{1,2,0:T(8,128)(2,1)S(1)} %convolution_convert_fusion), channel_id=2, replica_groups=mesh['dp'=4,'cand'=32,'tensor'=4] {'tensor'}, dimensions={0}, use_global_device_ids=true | all-gather | bytes 40960 | tf_op jit(solution)/shard_map/all_gather | solution.py:37
  137.2 0.7 collective-permute-start.1
  137.9 1.3 fusion.10
  139.2 11.4 %all-gather.10.cloned.1.call-done = bf16[3584,896]{1,0:T(8,128)(2,1)} async-done(((bf16[112,896]{1,0:T(8,128)(2,1)}), bf16[3584,896]{1,0:T(8,128)(2,1)}) %all-gather.10.cloned.1.call-update) | async-done | bytes 6422544 | tf_op jit(solution)/shard_map/all_gather | solution.py:33
  150.6 6.2 %fusion.7 = bf16[4,2,32,3584]{3,2,1,0:T(8,128)(2,1)} fusion(bf16[3584,896]{1,0:T(8,128)(2,1)} %all-gather.10.cloned.1.call-done, bf16[2,4,32,896]{3,2,1,0:T(8,128)(2,1)S(1)} %bitcast.85), kind=kOutput, calls=%fused_computation.5 | convolution fusion | flops 1645084672 | bytes 8716288 | tf_op jit(solution)/shard_map/tqch,dh->tqcd/dot_general | solution.py:69
  156.8 6.8 %all-to-all-start.2 = ((bf16[4,2,32,3584]{3,2,1,0:T(8,128)(2,1)}), bf16[4,2,32,3584]{3,2,1,0:T(8,128)(2,1)S(1)}, u32[]{:S(2)}, u32[]{:S(2)}) async-start(bf16[4,2,32,3584]{3,2,1,0:T(8,128)(2,1)} %fusion.7), calls=%async_computation.2 | async-start | bytes 3670016 | tf_op jit(solution)/shard_map/all_to_all | solution.py:72
  163.6 0.7 mul.141
  164.4 22.2 %all-to-all-done.2 = bf16[4,2,32,3584]{3,2,1,0:T(8,128)(2,1)S(1)} async-done(((bf16[4,2,32,3584]{3,2,1,0:T(8,128)(2,1)}), bf16[4,2,32,3584]{3,2,1,0:T(8,128)(2,1)S(1)}, u32[]{:S(2)}, u32[]{:S(2)}) %all-to-all-start.2) | async-done | bytes 1835040 | tf_op jit(solution)/shard_map/all_to_all | solution.py:72
  186.6 0.3 convert_reduce_fusion
  186.9 0.9 copy-done.2
  187.8 0.3 fusion.36
  188.1 1.3 fusion.39
  189.4 0.1 copy.56
  189.5 6.1 %all-gather.4 = f32[4,2,33]{2,1,0:T(2,128)S(1)} all-gather(f32[1,2,33]{2,1,0:T(2,128)S(1)} %maximum_bitcast_fusion.2), channel_id=3, replica_groups=mesh['dp'=4,'cand'=32,'tensor'=4] {'tensor'}, dimensions={0}, use_global_device_ids=true | all-gather | bytes 1320 | tf_op jit(solution)/shard_map/all_gather | solution.py:83
  195.7 0.1 sub.37
  195.7 0.2 slice_reduce_fusion.1
  195.9 0.1 copy.58
  196.0 34.3 %all-gather.5 = f32[32,2,129]{2,1,0:T(2,128)S(1)} all-gather(f32[1,2,129]{2,1,0:T(2,128)S(1)} %maximum_bitcast_fusion.1), channel_id=4, replica_groups=mesh['dp'=4,'cand'=32,'tensor'=4] {'cand'}, dimensions={0}, use_global_device_ids=true | all-gather | bytes 34056 | tf_op jit(solution)/shard_map/all_gather | solution.py:86
  230.4 1.1 fusion.35
  231.5 0.1 copy.60
  231.6 0.1 slice_reduce_fusion
  231.8 6.6 %psum.7 = f32[2,129]{1,0:T(2,128)S(1)} all-reduce(f32[2,129]{1,0:T(2,128)S(1)} %pad_maximum_fusion), channel_id=1, replica_groups=mesh['dp'=4,'cand'=32,'tensor'=4] {'tensor'}, use_global_device_ids=true, to_apply=%region_11.12 | all-reduce | flops 258 | bytes 2064 | tf_op jit(solution)/shard_map/psum | solution.py:93
  238.4 0.1 slice_reduce_fusion.2
  238.5 0.2 dynamic_update_slice.3
  238.9 2.1 multiply_convert_fusion.1
  241.0 2.2 fusion.44
  243.2 0.4 fusion.48
  243.6 0.2 convolution_bitcast_fusion.1
  243.7 0.3 fusion.20
  244.0 0.8 copy.61
  244.8 9.0 %all-to-all-start.3 = ((f32[32,1,1024]{2,1,0:T(1,128)}), f32[32,1,1024]{2,1,0:T(1,128)S(1)}, u32[]{:S(2)}, u32[]{:S(2)}) async-start(f32[32,1,1024]{2,1,0:T(1,128)} %copy.61), calls=%async_computation.3 | async-start | bytes 262144 | tf_op jit(solution)/shard_map/all_to_all | solution.py:118
  253.8 5.7 %fusion.17 = bf16[2,128,896]{2,1,0:T(8,128)(2,1)} fusion(f32[2,128,896]{2,1,0:T(8,128)S(1)} %fusion.48, bf16[2,128,3584]{2,1,0:T(8,128)(2,1)S(1)} %copy-done.3, bf16[3584,896]{1,0:T(8,128)(2,1)} %all-gather.10.cloned.1.call-done, f32[2,128]{1,0:T(2,128)S(1)} %get-tuple-element.31), kind=kOutput, calls=%fused_computation.22 | convolution fusion | flops 1644855296 | bytes 9634816 | tf_op jit(solution)/shard_map/qcd,dh->qch/dot_general | solution.py:100
  259.5 10.2 %all-to-all-done.3 = f32[32,1,1024]{2,1,0:T(1,128)S(1)} async-done(((f32[32,1,1024]{2,1,0:T(1,128)}), f32[32,1,1024]{2,1,0:T(1,128)S(1)}, u32[]{:S(2)}, u32[]{:S(2)}) %all-to-all-start.3) | async-done | bytes 131104 | tf_op jit(solution)/shard_map/all_to_all | solution.py:118
  269.7 0.1 reduce_sum.143
  269.8 9.4 %all-gather.3 = f32[4096]{0:T(1024)S(1)} all-gather(f32[1024]{0:T(1024)S(1)} %reduce_sum.143), channel_id=5, replica_groups=mesh['dp'=4,'cand'=32,'tensor'=4] {'dp'}, dimensions={0}, use_global_device_ids=true | all-gather | bytes 20480 | tf_op jit(solution)/shard_map/all_gather | solution.py:120
  279.2 0.6 fusion.57
  279.8 31.7 %all-gather.6 = f32[32,1,896]{2,1,0:T(1,128)S(1)} all-gather(f32[1,1,896]{2,1,0:T(1,128)S(1)} %slice_bitcast_fusion.1), channel_id=1, replica_groups=mesh['dp'=4,'cand'=32,'tensor'=4] {'cand'}, dimensions={0}, use_global_device_ids=true | all-gather | bytes 118272 | tf_op jit(solution)/shard_map/all_gather | solution.py:121
  311.5 0.6 copy_bitcast_fusion
  (51 shorter events, 0.6 us)
Async XLA Ops:
  7.2 130.7 %copy-start = (bf16[16,3584]{1,0:T(8,128)(2,1)S(1)}, bf16[16,3584]{1,0:T(8,128)(2,1)}, u32[]{:S(2)}) copy-start(bf16[16,3584]{1,0:T(8,128)(2,1)} %param.14) | copy-start | bytes 344068
  7.2 143.4 %all-gather.10.cloned.1.call-start = ((), (), s32[]{:S(2)}) async-start(), calls=%async_computation.4 | async-start | bytes 6623232 | tf_op jit(solution)/shard_map/all_gather | solution.py:33
  9.6 26.4 %copy-start.6 = (bf16[2,128,1024]{2,1,0:T(8,128)(2,1)S(1)}, bf16[2,128,1024]{2,1,0:T(8,128)(2,1)}, u32[]{:S(2)}) copy-start(bf16[2,128,1024]{2,1,0:T(8,128)(2,1)} %param.17) | copy-start | bytes 1572868
  34.3 2.0 collective-permute-start
  36.3 6.3 %copy-start.4 = (bf16[2,128,896]{2,1,0:T(8,128)(2,1)S(1)}, bf16[2,128,896]{2,1,0:T(8,128)(2,1)}, u32[]{:S(2)}) copy-start(bf16[2,128,896]{2,1,0:T(8,128)(2,1)} %param.10) | copy-start | bytes 1376260
  36.3 6.3 %copy-start.8 = (bf16[896,16]{0,1:T(8,128)(2,1)S(1)}, bf16[896,16]{0,1:T(8,128)(2,1)}, u32[]{:S(2)}) copy-start(bf16[896,16]{0,1:T(8,128)(2,1)} %param.13) | copy-start | bytes 86020
  36.3 101.6 %copy-start.7 = (bf16[2,32,3584]{2,1,0:T(8,128)(2,1)S(1)}, bf16[2,32,3584]{2,1,0:T(8,128)(2,1)}, u32[]{:S(2)}) copy-start(bf16[2,32,3584]{2,1,0:T(8,128)(2,1)} %param.11) | copy-start | bytes 1376260
  38.3 98.9 %all-to-all-start.1 = ((f32[8,2,128]{2,1,0:T(2,128)}), f32[8,2,128]{2,1,0:T(2,128)S(1)}, u32[]{:S(2)}, u32[]{:S(2)}) async-start(f32[8,2,128]{2,1,0:T(2,128)} %bitcast.8), calls=%async_computation.1 | async-start | bytes 16384 | tf_op jit(solution)/shard_map/all_to_all | solution.py:61
  137.2 2.0 collective-permute-start.1
  156.8 29.8 %all-to-all-start.2 = ((bf16[4,2,32,3584]{3,2,1,0:T(8,128)(2,1)}), bf16[4,2,32,3584]{3,2,1,0:T(8,128)(2,1)S(1)}, u32[]{:S(2)}, u32[]{:S(2)}) async-start(bf16[4,2,32,3584]{3,2,1,0:T(8,128)(2,1)} %fusion.7), calls=%async_computation.2 | async-start | bytes 3670016 | tf_op jit(solution)/shard_map/all_to_all | solution.py:72
  163.6 77.4 %all-gather.12.cloned.1.call-start = ((), (), s32[]{:S(2)}) async-start(), calls=%async_computation.5 | async-start | bytes 2293760 | tf_op jit(solution)/shard_map/all_gather | solution.py:81
  186.6 1.2 copy-start.2
  187.8 42.6 %copy-start.1 = (f32[2,128,1024]{1,2,0:T(8,128)S(1)}, f32[2,128,1024]{1,2,0:T(8,128)}, u32[]{:S(2)}) copy-start(f32[2,128,1024]{1,2,0:T(8,128)} %get-tuple-element.14) | copy-start | bytes 3145732
  189.3 42.4 %copy-start.10 = (f32[2]{0:T(128)S(1)}, f32[2]{0:T(128)}, u32[]{:S(2)}) copy-start(f32[2]{0:T(128)} %param.19) | copy-start | bytes 28
  231.5 11.7 %copy-start.9 = (bf16[896,16]{0,1:T(8,128)(2,1)S(1)}, bf16[896,16]{0,1:T(8,128)(2,1)}, u32[]{:S(2)}) copy-start(bf16[896,16]{0,1:T(8,128)(2,1)} %param.13) | copy-start | bytes 86020
  238.9 4.7 %copy-start.5 = (bf16[2,128,896]{2,1,0:T(8,128)(2,1)S(1)}, bf16[2,128,896]{2,1,0:T(8,128)(2,1)}, u32[]{:S(2)}) copy-start(bf16[2,128,896]{2,1,0:T(8,128)(2,1)} %param.10) | copy-start | bytes 1376260
  241.0 2.7 copy-start.3
  244.8 24.9 %all-to-all-start.3 = ((f32[32,1,1024]{2,1,0:T(1,128)}), f32[32,1,1024]{2,1,0:T(1,128)S(1)}, u32[]{:S(2)}, u32[]{:S(2)}) async-start(f32[32,1,1024]{2,1,0:T(1,128)} %copy.61), calls=%async_computation.3 | async-start | bytes 262144 | tf_op jit(solution)/shard_map/all_to_all | solution.py:118
Sparse Core Ops, SparseCore 0:
  10.1 140.4 all-gather.9
  189.5 34.1 all-gather.11
